TPU v7x, 32 devices: a whole 2x2x4 slice. The times are simulated.
32 devices in a mesh: gx: 8 (over z, core), gy: 4 (over y, x).
Axes of the slice: x: 2, y: 2, z: 4, core: 2. Of those that a mesh axis runs over, the one named last changes fastest.
Arguments:
- load: float32 [8, 4, 320, 768], P('gx', 'gy'), may hold values from -6 to 6
- stiffness: bfloat16 [8, 4, 768, 768], P('gx', 'gy'), may hold values from -0.5 to 3, as said below
- local_inverse: bfloat16 [8, 4, 768, 768], P('gx', 'gy'), may hold values from -0.5 to 3, as said below
- phi: float32 [8, 4, 8, 768], P('gx', 'gy'), may hold values from -2.5 to 2.5
- level2_inverse: float32 [8, 32, 32], P('gx'), may hold values from -0.5 to 3, as said below
- level3_inverse: bfloat16 [128, 128], replicated, may hold values from -0.5 to 3, as said below
- aggregate: int32 [8, 4], P('gx', 'gy'), may hold values from 0 to 1
Outputs:
- solution: float32 [8, 4, 320, 768], P('gx', 'gy')
Inputs may be any that keep to these rules, and one draw needn't show every extreme that they name: `stiffness`: every block is symmetric positive definite. `local_inverse`: every block is symmetric positive definite. `level2_inverse`: every block is symmetric positive definite. `level3_inverse`: symmetric positive definite.
All inputs are finite; a program needn't handle non-finite values.
Results may differ from a plain program's by a relative error of at most 0.0091.
Values may be sent and summed in bfloat16 or wider, within the bound.
A program may use at most 64 MiB of HBM per device.

v0:
```python
import jax
import jax.numpy as jnp
from jax import lax
from jax.sharding import PartitionSpec as P

NAGG = 2
ITERS = 2


HIGH = lax.Precision.HIGHEST


def from_behind(value, axis, steps):
    count = lax.axis_size(axis)
    first, last = (max(0, -steps), min(count, count - steps))
    return lax.ppermute(value, axis, [(source, source + steps) for source in range(first, last)])


def assemble(vec):
    rows, total = vec.shape
    width = total // 4
    edges = vec.reshape(rows, 4, width)
    west, east, south, north = (edges[:, 0], edges[:, 1], edges[:, 2], edges[:, 3])
    new_west = west + from_behind(east, "gx", 1)
    new_east = east + from_behind(west, "gx", -1)
    new_south = south + from_behind(north, "gy", 1)
    new_north = north + from_behind(south, "gy", -1)
    return jnp.stack([new_west, new_east, new_south, new_north], axis=1).reshape(rows, total)


def contract_last(left, right):
    return lax.dot_general(
        left, right, (((1,), (1,)), ((), ())), preferred_element_type=jnp.float32
    )


def contract_high(left, right):
    return lax.dot_general(
        left, right, (((1,), (1,)), ((), ())), precision=HIGH, preferred_element_type=jnp.float32
    )


def body(load, stiffness, local_inverse, phi, level2_inverse, level3_inverse, aggregate):
    load_here = load[0, 0]
    stiff = stiffness[0, 0]
    inverse = local_inverse[0, 0]
    basis = phi[0, 0]
    second_inv = level2_inverse[0]
    rows, total = load_here.shape
    width = total // 4
    primal_count = basis.shape[0]
    block = NAGG * primal_count
    col = lax.axis_index("gx")
    row = lax.axis_index("gy")
    cols_total = lax.axis_size("gx")
    rows_total = lax.axis_size("gy")
    edge_w = jnp.stack(
        [
            jnp.where(col > 0, 0.5, 1.0),
            jnp.where(col < cols_total - 1, 0.5, 1.0),
            jnp.where(row > 0, 0.5, 1.0),
            jnp.where(row < rows_total - 1, 0.5, 1.0),
        ]
    ).astype(jnp.float32)
    weights = jnp.repeat(edge_w, width)
    labels = jnp.arange(NAGG, dtype=jnp.int32)
    own_onehot = (aggregate[0, 0] == labels).astype(jnp.float32)
    members = lax.all_gather(aggregate[0], "gy", axis=0, tiled=True)
    group_onehot = (members[:, None] == labels[None, :]).astype(jnp.float32)

    def apply(vec):
        return assemble(contract_last(vec.astype(jnp.bfloat16), stiff))

    def precondition(resid):
        scaled = weights * resid
        local = contract_last(scaled.astype(jnp.bfloat16), inverse)
        primal = contract_high(scaled, basis)
        grouped = lax.all_gather(primal, "gy", axis=1, tiled=True)
        summed = jnp.einsum(
            "rbp,bq->rqp",
            grouped.reshape(rows, rows_total, primal_count),
            group_onehot,
            precision=HIGH,
        )
        summed = summed.reshape(rows, block)
        summed = summed.astype(jnp.bfloat16)
        second = contract_high(grouped, second_inv)
        second_own = lax.dynamic_slice_in_dim(second, row * primal_count, primal_count, 1)
        everyone = lax.all_gather(summed, "gx", axis=1, tiled=True)
        mine = lax.dynamic_slice_in_dim(level3_inverse, col * block, block, 0)
        third = contract_last(everyone, mine)
        third_own = jnp.einsum(
            "rqp,q->rp", third.reshape(rows, NAGG, primal_count), own_onehot, precision=HIGH
        )
        full = local + jnp.dot(
            second_own + third_own, basis, precision=HIGH, preferred_element_type=jnp.float32
        )
        return assemble(weights * full)

    def inner(left, right):
        return jnp.sum(weights * left * right, axis=1)

    rhs = assemble(load_here)
    solution = jnp.zeros_like(rhs)
    resid = rhs

    def paired(resid, zvec, wvec):
        return lax.psum((inner(resid, zvec), inner(zvec, wvec)), ("gx", "gy"))

    zvec = precondition(resid)
    wvec = apply(zvec)
    gamma, delta = paired(resid, zvec, wvec)
    alpha = gamma / delta
    pvec, svec = (zvec, wvec)
    for step in range(ITERS):
        solution = solution + alpha[:, None] * pvec
        resid = resid - alpha[:, None] * svec
        if step < ITERS - 1:
            zvec = precondition(resid)
            wvec = apply(zvec)
            newer, delta = paired(resid, zvec, wvec)
            beta = newer / gamma
            alpha = newer / (delta - beta * newer / alpha)
            pvec = zvec + beta[:, None] * pvec
            svec = wvec + beta[:, None] * svec
            gamma = newer
    return solution[None, None]


def solution(mesh):
    return jax.shard_map(
        body,
        mesh=mesh,
        in_specs=(
            P("gx", "gy", None, None),
            P("gx", "gy", None, None),
            P("gx", "gy", None, None),
            P("gx", "gy", None, None),
            P("gx", None, None),
            P(),
            P("gx", "gy"),
        ),
        out_specs=P("gx", "gy", None, None),
        check_vma=False,
    )
```

profile of v0, /device:TPU:0, one launch (start us, length us, event | category | flops | bytes accessed | tf_op | source)
XLA Modules:
  0.0 265.9 jit_solution(13401014235180399910)
XLA Ops:
  0.0 1.7 copy.24
  1.7 1.0 slice_bitcast_fusion.18
  2.6 2.4 collective-permute-start
  5.0 4.2 %collective-permute-start.2 = (f32[320,192]{0,1:T(8,128)}, f32[320,192]{0,1:T(8,128)S(1)}, u32[]{:S(2)}, u32[]{:S(2)}) collective-permute-start(f32[320,192]{0,1:T(8,128)} %get-tuple-element.58), channel_id=1, source_target_pairs={{0,1},{1,2},{2,3},{4,5},{5,6},{6,7},{8,9},{9,10},{10,11},{12,13},{... | collective-permute-start | bytes 737288 | tf_op jit(solution)/shard_map/ppermute | solution.py:16
  9.3 1.3 collective-permute-start.3
  10.6 1.3 collective-permute-start.1
  13.8 12.4 %all-reduce = s32[4]{0:T(128)} all-reduce(s32[4]{0:T(128)S(1)} %bitcast_dynamic-update-slice_fusion), channel_id=2, replica_groups=mesh['gx'=8,'gy'=4] {'gy'}, use_global_device_ids=true, to_apply=%add | all-reduce | flops 4 | bytes 32
  26.4 0.7 mul.183
  27.1 1.1 add_bitcast_fusion.19
  28.2 1.1 fusion.43
  29.4 0.7 fusion.18
  30.1 9.1 %all_gather.15 = f32[320,32]{0,1:T(8,128)S(1)} all-gather(f32[320,8]{0,1:T(8,128)S(1)} %fusion.18), channel_id=1, replica_groups=mesh['gx'=8,'gy'=4] {'gy'}, dimensions={1}, use_global_device_ids=true | all-gather | bytes 51200 | tf_op jit(solution)/shard_map/all_gather | solution.py:78
  40.0 14.4 %all_gather.17 = bf16[320,128]{0,1:T(8,128)(2,1)S(1)} all-gather(bf16[320,16]{0,1:T(8,128)(2,1)S(1)} %bitcast.227), channel_id=1, replica_groups=mesh['gx'=8,'gy'=4] {'gx'}, dimensions={1}, use_global_device_ids=true | all-gather | bytes 92160 | tf_op jit(solution)/shard_map/all_gather | solution.py:89
  54.5 0.8 convolution_bitcast_fusion.1
  55.3 0.8 fusion.22
  56.1 1.5 copy.37
  57.6 1.2 fusion.26
  58.9 1.8 fusion.5
  60.7 1.9 fusion.1
  62.6 1.6 copy.27
  64.3 2.3 collective-permute-start.4
  66.6 1.9 collective-permute-start.6
  68.5 1.3 collective-permute-start.7
  69.8 1.3 collective-permute-start.5
  71.1 4.1 %collective-permute-done.6 = f32[320,192]{0,1:T(8,128)S(1)} collective-permute-done((f32[320,192]{0,1:T(8,128)S(1)}, f32[320,192]{0,1:T(8,128)S(1)}, u32[]{:S(2)}, u32[]{:S(2)}) %collective-permute-start.6) | collective-permute-done | bytes 245792 | tf_op jit(solution)/shard_map/ppermute | solution.py:16
  75.2 8.2 %collective-permute-done.7 = f32[320,192]{0,1:T(8,128)S(1)} collective-permute-done((f32[320,192]{0,1:T(8,128)S(1)}, f32[320,192]{0,1:T(8,128)S(1)}, u32[]{:S(2)}, u32[]{:S(2)}) %collective-permute-start.7) | collective-permute-done | bytes 245792 | tf_op jit(solution)/shard_map/ppermute | solution.py:16
  83.7 0.8 fusion.45
  84.6 1.3 collective-permute-start.8
  86.0 4.0 %collective-permute-start.10 = (f32[320,192]{0,1:T(8,128)S(1)}, f32[320,192]{0,1:T(8,128)S(1)}, u32[]{:S(2)}, u32[]{:S(2)}) collective-permute-start(f32[320,192]{0,1:T(8,128)S(1)} %get-tuple-element.42), channel_id=1, source_target_pairs={{0,1},{1,2},{2,3},{4,5},{5,6},{6,7},{8,9},{9,10},{10,11},{12,13},{... | collective-permute-start | bytes 737288 | tf_op jit(solution)/shard_map/ppermute | solution.py:16
  89.9 1.3 collective-permute-start.11
  91.3 1.3 collective-permute-start.9
  92.6 4.4 %collective-permute-done.10 = f32[320,192]{0,1:T(8,128)S(1)} collective-permute-done((f32[320,192]{0,1:T(8,128)S(1)}, f32[320,192]{0,1:T(8,128)S(1)}, u32[]{:S(2)}, u32[]{:S(2)}) %collective-permute-start.10) | collective-permute-done | bytes 245792 | tf_op jit(solution)/shard_map/ppermute | solution.py:16
  97.0 6.5 %collective-permute-done.11 = f32[320,192]{0,1:T(8,128)S(1)} collective-permute-done((f32[320,192]{0,1:T(8,128)S(1)}, f32[320,192]{0,1:T(8,128)S(1)}, u32[]{:S(2)}, u32[]{:S(2)}) %collective-permute-start.11) | collective-permute-done | bytes 245792 | tf_op jit(solution)/shard_map/ppermute | solution.py:16
  103.7 2.0 multiply_reduce_fusion.1
  105.7 39.3 %all-reduce.2 = (f32[320]{0:T(512)S(1)}, f32[320]{0:T(512)S(1)}) all-reduce(f32[320]{0:T(512)} %get-tuple-element.8, f32[320]{0:T(512)} %get-tuple-element.7), channel_id=1, replica_groups=mesh['gx'=8,'gy'=4] {'gx','gy'}, use_global_device_ids=true, to_apply=%region_1.2 | all-reduce | flops 640 | bytes 5120 | tf_op jit(solution)/shard_map/psum | solution.py:108
  145.7 2.4 fusion.42
  148.2 0.7 fusion.15
  148.8 9.0 %all_gather.18 = f32[320,32]{0,1:T(8,128)S(1)} all-gather(f32[320,8]{0,1:T(8,128)S(1)} %fusion.15), channel_id=1, replica_groups=mesh['gx'=8,'gy'=4] {'gy'}, dimensions={1}, use_global_device_ids=true | all-gather | bytes 51200 | tf_op jit(solution)/shard_map/all_gather | solution.py:78
  157.9 1.1 fusion.24
  159.2 14.1 %all_gather.19 = bf16[320,128]{0,1:T(8,128)(2,1)S(1)} all-gather(bf16[320,16]{0,1:T(8,128)(2,1)S(1)} %bitcast.228), channel_id=1, replica_groups=mesh['gx'=8,'gy'=4] {'gx'}, dimensions={1}, use_global_device_ids=true | all-gather | bytes 92160 | tf_op jit(solution)/shard_map/all_gather | solution.py:89
  173.3 0.8 convolution_bitcast_fusion
  174.3 0.8 copy.40
  175.1 1.8 fusion.3
  176.9 1.9 fusion
  178.9 1.6 copy.32
  180.5 2.3 collective-permute-start.12
  182.8 1.9 collective-permute-start.14
  184.8 1.3 collective-permute-start.15
  186.1 1.3 collective-permute-start.13
  187.4 3.9 %collective-permute-done.14 = f32[320,192]{0,1:T(8,128)S(1)} collective-permute-done((f32[320,192]{0,1:T(8,128)S(1)}, f32[320,192]{0,1:T(8,128)S(1)}, u32[]{:S(2)}, u32[]{:S(2)}) %collective-permute-start.14) | collective-permute-done | bytes 245792 | tf_op jit(solution)/shard_map/ppermute | solution.py:16
  191.3 8.2 %collective-permute-done.15 = f32[320,192]{0,1:T(8,128)S(1)} collective-permute-done((f32[320,192]{0,1:T(8,128)S(1)}, f32[320,192]{0,1:T(8,128)S(1)}, u32[]{:S(2)}, u32[]{:S(2)}) %collective-permute-start.15) | collective-permute-done | bytes 245792 | tf_op jit(solution)/shard_map/ppermute | solution.py:16
  199.9 0.8 fusion.46
  200.8 1.0 slice_bitcast_fusion.2
  201.8 2.0 collective-permute-start.16
  203.8 4.5 %collective-permute-start.18 = (f32[320,192]{0,1:T(8,128)}, f32[320,192]{0,1:T(8,128)}, u32[]{:S(2)}, u32[]{:S(2)}) collective-permute-start(f32[320,192]{0,1:T(8,128)} %get-tuple-element.25), channel_id=1, source_target_pairs={{0,1},{1,2},{2,3},{4,5},{5,6},{6,7},{8,9},{9,10},{10,11},{12,13},{... | collective-permute-start | bytes 737288 | tf_op jit(solution)/shard_map/ppermute | solution.py:16
  208.3 1.3 collective-permute-start.19
  209.5 1.3 collective-permute-start.17
  210.8 2.6 copy.29
  213.5 1.7 collective-permute-done.18
  215.2 6.6 %collective-permute-done.19 = f32[320,192]{0,1:T(8,128)} collective-permute-done((f32[320,192]{0,1:T(8,128)}, f32[320,192]{0,1:T(8,128)}, u32[]{:S(2)}, u32[]{:S(2)}) %collective-permute-start.19) | collective-permute-done | bytes 245792 | tf_op jit(solution)/shard_map/ppermute | solution.py:16
  221.8 1.3 add_bitcast_fusion.3
  223.6 1.3 copy.35
  224.9 38.5 %all-reduce.1 = (f32[320]{0:T(512)S(1)}, f32[320]{0:T(512)S(1)}) all-reduce(f32[320]{0:T(512)S(1)} %get-tuple-element.6, f32[320]{0:T(512)S(1)} %get-tuple-element.5), channel_id=1, replica_groups=mesh['gx'=8,'gy'=4] {'gx','gy'}, use_global_device_ids=true, to_apply=%region_5.6 | all-reduce | flops 640 | bytes 5120 | tf_op jit(solution)/shard_map/psum | solution.py:108
  263.5 2.4 multiply_add_fusion
  (127 shorter events, 4.8 us)
Async XLA Ops:
  0.0 83.7 %copy-start = (bf16[1,1,768,768]{3,2,1,0:T(8,128)(2,1)S(1)}, bf16[1,1,768,768]{3,2,1,0:T(8,128)(2,1)}, u32[]{:S(2)}) copy-start(bf16[1,1,768,768]{3,2,1,0:T(8,128)(2,1)} %param.8) | copy-start | bytes 3538948
  1.7 10.9 %copy-start.46 = (u32[32]{0:T(128)S(1)}, u32[32]{0:T(128)}, u32[]{:S(2)}) copy-start(u32[32]{0:T(128)} %constant.37) | copy-start | bytes 388
  2.6 24.4 %collective-permute-start = (f32[320,192]{0,1:T(8,128)}, f32[320,192]{0,1:T(8,128)S(1)}, u32[]{:S(2)}, u32[]{:S(2)}) collective-permute-start(f32[320,192]{0,1:T(8,128)} %get-tuple-element.57), channel_id=1, source_target_pairs={{0,4},{4,8},{8,12},{12,16},{16,20},{20,24},{24,28},{1,5},{5,9},{9,... | collective-permute-start | bytes 737288 | tf_op jit(solution)/shard_map/ppermute | solution.py:16
  5.0 22.0 %collective-permute-start.2 = (f32[320,192]{0,1:T(8,128)}, f32[320,192]{0,1:T(8,128)S(1)}, u32[]{:S(2)}, u32[]{:S(2)}) collective-permute-start(f32[320,192]{0,1:T(8,128)} %get-tuple-element.58), channel_id=1, source_target_pairs={{0,1},{1,2},{2,3},{4,5},{5,6},{6,7},{8,9},{9,10},{10,11},{12,13},{... | collective-permute-start | bytes 737288 | tf_op jit(solution)/shard_map/ppermute | solution.py:16
  9.3 17.8 %collective-permute-start.3 = (f32[320,192]{0,1:T(8,128)}, f32[320,192]{0,1:T(8,128)S(1)}, u32[]{:S(2)}, u32[]{:S(2)}) collective-permute-start(f32[320,192]{0,1:T(8,128)} %get-tuple-element.59), channel_id=1, source_target_pairs={{1,0},{2,1},{3,2},{5,4},{6,5},{7,6},{9,8},{10,9},{11,10},{13,12},{... | collective-permute-start | bytes 737288 | tf_op jit(solution)/shard_map/ppermute | solution.py:16
  10.6 16.5 %collective-permute-start.1 = (f32[320,192]{0,1:T(8,128)S(1)}, f32[320,192]{0,1:T(8,128)}, u32[]{:S(2)}, u32[]{:S(2)}) collective-permute-start(f32[320,192]{0,1:T(8,128)S(1)} %get-tuple-element.60), channel_id=1, source_target_pairs={{4,0},{8,4},{12,8},{16,12},{20,16},{24,20},{28,24},{5,1},{9,5},{13... | collective-permute-start | bytes 737288 | tf_op jit(solution)/shard_map/ppermute | solution.py:16
  26.3 1.9 copy-start.37
  28.2 1.2 copy-start.12
  28.2 1.2 copy-start.14
  28.2 1.2 copy-start.16
  28.2 1.2 copy-start.18
  28.2 1.2 copy-start.28
  29.4 10.5 %copy-start.44 = (s32[4]{0:T(128)S(1)}, s32[4]{0:T(128)}, u32[]{:S(2)}) copy-start(s32[4]{0:T(128)} %all-reduce) | copy-start | bytes 52
  29.4 28.2 %copy-start.32 = (f32[1,32,32]{2,1,0:T(8,128)S(1)}, f32[1,32,32]{2,1,0:T(8,128)}, u32[]{:S(2)}) copy-start(f32[1,32,32]{2,1,0:T(8,128)} %param.11) | copy-start | bytes 12292
  29.4 29.4 %copy-start.1 = (bf16[1,1,768,768]{3,2,1,0:T(8,128)(2,1)S(1)}, bf16[1,1,768,768]{3,2,1,0:T(8,128)(2,1)}, u32[]{:S(2)}) copy-start(bf16[1,1,768,768]{3,2,1,0:T(8,128)(2,1)} %param.9) | copy-start | bytes 3538948
  58.8 1.8 copy-start.26
  58.9 1.8 copy-start.29
  58.9 1.8 copy-start.33
  64.3 6.8 %collective-permute-start.4 = (f32[320,192]{0,1:T(8,128)S(1)}, f32[320,192]{0,1:T(8,128)S(1)}, u32[]{:S(2)}, u32[]{:S(2)}) collective-permute-start(f32[320,192]{0,1:T(8,128)S(1)} %get-tuple-element.49), channel_id=1, source_target_pairs={{0,4},{4,8},{8,12},{12,16},{16,20},{20,24},{24,28},{1,5},{5,9},{9,... | collective-permute-start | bytes 737288 | tf_op jit(solution)/shard_map/ppermute | solution.py:16
  66.6 8.6 %collective-permute-start.6 = (f32[320,192]{0,1:T(8,128)S(1)}, f32[320,192]{0,1:T(8,128)S(1)}, u32[]{:S(2)}, u32[]{:S(2)}) collective-permute-start(f32[320,192]{0,1:T(8,128)S(1)} %get-tuple-element.50), channel_id=1, source_target_pairs={{0,1},{1,2},{2,3},{4,5},{5,6},{6,7},{8,9},{9,10},{10,11},{12,13},{... | collective-permute-start | bytes 737288 | tf_op jit(solution)/shard_map/ppermute | solution.py:16
  68.5 14.9 %collective-permute-start.7 = (f32[320,192]{0,1:T(8,128)S(1)}, f32[320,192]{0,1:T(8,128)S(1)}, u32[]{:S(2)}, u32[]{:S(2)}) collective-permute-start(f32[320,192]{0,1:T(8,128)S(1)} %get-tuple-element.51), channel_id=1, source_target_pairs={{1,0},{2,1},{3,2},{5,4},{6,5},{7,6},{9,8},{10,9},{11,10},{13,12},{... | collective-permute-start | bytes 737288 | tf_op jit(solution)/shard_map/ppermute | solution.py:16
  69.8 13.6 %collective-permute-start.5 = (f32[320,192]{0,1:T(8,128)S(1)}, f32[320,192]{0,1:T(8,128)S(1)}, u32[]{:S(2)}, u32[]{:S(2)}) collective-permute-start(f32[320,192]{0,1:T(8,128)S(1)} %get-tuple-element.52), channel_id=1, source_target_pairs={{4,0},{8,4},{12,8},{16,12},{20,16},{24,20},{28,24},{5,1},{9,5},{13... | collective-permute-start | bytes 737288 | tf_op jit(solution)/shard_map/ppermute | solution.py:16
  84.6 7.9 %collective-permute-start.8 = (f32[320,192]{0,1:T(8,128)S(1)}, f32[320,192]{0,1:T(8,128)S(1)}, u32[]{:S(2)}, u32[]{:S(2)}) collective-permute-start(f32[320,192]{0,1:T(8,128)S(1)} %get-tuple-element.41), channel_id=1, source_target_pairs={{0,4},{4,8},{8,12},{12,16},{16,20},{20,24},{24,28},{1,5},{5,9},{9,... | collective-permute-start | bytes 737288 | tf_op jit(solution)/shard_map/ppermute | solution.py:16
  86.0 11.0 %collective-permute-start.10 = (f32[320,192]{0,1:T(8,128)S(1)}, f32[320,192]{0,1:T(8,128)S(1)}, u32[]{:S(2)}, u32[]{:S(2)}) collective-permute-start(f32[320,192]{0,1:T(8,128)S(1)} %get-tuple-element.42), channel_id=1, source_target_pairs={{0,1},{1,2},{2,3},{4,5},{5,6},{6,7},{8,9},{9,10},{10,11},{12,13},{... | collective-permute-start | bytes 737288 | tf_op jit(solution)/shard_map/ppermute | solution.py:16
  89.9 13.6 %collective-permute-start.11 = (f32[320,192]{0,1:T(8,128)S(1)}, f32[320,192]{0,1:T(8,128)S(1)}, u32[]{:S(2)}, u32[]{:S(2)}) collective-permute-start(f32[320,192]{0,1:T(8,128)S(1)} %get-tuple-element.43), channel_id=1, source_target_pairs={{1,0},{2,1},{3,2},{5,4},{6,5},{7,6},{9,8},{10,9},{11,10},{13,12},{... | collective-permute-start | bytes 737288 | tf_op jit(solution)/shard_map/ppermute | solution.py:16
  91.2 12.4 %copy-start.38 = (f32[4]{0:T(128)S(1)}, f32[4]{0:T(128)}, u32[]{:S(2)}) copy-start(f32[4]{0:T(128)} %copy-done.37) | copy-start | bytes 52
  91.3 12.2 %collective-permute-start.9 = (f32[320,192]{0,1:T(8,128)S(1)}, f32[320,192]{0,1:T(8,128)S(1)}, u32[]{:S(2)}, u32[]{:S(2)}) collective-permute-start(f32[320,192]{0,1:T(8,128)S(1)} %get-tuple-element.44), channel_id=1, source_target_pairs={{4,0},{8,4},{12,8},{16,12},{20,16},{24,20},{28,24},{5,1},{9,5},{13... | collective-permute-start | bytes 737288 | tf_op jit(solution)/shard_map/ppermute | solution.py:16
  103.6 2.1 copy-start.20
  103.6 2.1 copy-start.21
  103.6 2.1 copy-start.22
  103.6 2.1 copy-start.23
  103.7 42.0 %copy-start.13 = (f32[320,1,192]{0,2,1:T(8,128)S(1)}, f32[320,1,192]{0,2,1:T(8,128)}, u32[]{:S(2)}) copy-start(f32[320,1,192]{0,2,1:T(8,128)} %copy-done.12) | copy-start | bytes 737284
  103.7 42.0 %copy-start.15 = (f32[320,1,192]{0,2,1:T(8,128)S(1)}, f32[320,1,192]{0,2,1:T(8,128)}, u32[]{:S(2)}) copy-start(f32[320,1,192]{0,2,1:T(8,128)} %copy-done.14) | copy-start | bytes 737284
  103.7 42.0 %copy-start.17 = (f32[320,1,192]{0,2,1:T(8,128)S(1)}, f32[320,1,192]{0,2,1:T(8,128)}, u32[]{:S(2)}) copy-start(f32[320,1,192]{0,2,1:T(8,128)} %copy-done.16) | copy-start | bytes 737284
  103.7 42.0 %copy-start.19 = (f32[320,1,192]{0,2,1:T(8,128)S(1)}, f32[320,1,192]{0,2,1:T(8,128)}, u32[]{:S(2)}) copy-start(f32[320,1,192]{0,2,1:T(8,128)} %copy-done.18) | copy-start | bytes 737284
  145.7 2.4 copy-start.35
  145.7 2.4 copy-start.30
  148.1 10.9 %copy-start.45 = (s32[4]{0:T(128)S(1)}, s32[4]{0:T(128)}, u32[]{:S(2)}) copy-start(s32[4]{0:T(128)} %all-reduce) | copy-start | bytes 52
  148.1 27.0 %copy-start.2 = (bf16[1,1,768,768]{3,2,1,0:T(8,128)(2,1)S(1)}, bf16[1,1,768,768]{3,2,1,0:T(8,128)(2,1)}, u32[]{:S(2)}) copy-start(bf16[1,1,768,768]{3,2,1,0:T(8,128)(2,1)} %param.9) | copy-start | bytes 3538948
  175.1 1.8 copy-start.24
  175.1 1.8 copy-start.25
  175.1 1.8 copy-start.31
  175.1 1.8 copy-start.34
  180.5 6.8 %collective-permute-start.12 = (f32[320,192]{0,1:T(8,128)S(1)}, f32[320,192]{0,1:T(8,128)S(1)}, u32[]{:S(2)}, u32[]{:S(2)}) collective-permute-start(f32[320,192]{0,1:T(8,128)S(1)} %get-tuple-element.33), channel_id=1, source_target_pairs={{0,4},{4,8},{8,12},{12,16},{16,20},{20,24},{24,28},{1,5},{5,9},{9,... | collective-permute-start | bytes 737288 | tf_op jit(solution)/shard_map/ppermute | solution.py:16
  182.8 8.5 %collective-permute-start.14 = (f32[320,192]{0,1:T(8,128)S(1)}, f32[320,192]{0,1:T(8,128)S(1)}, u32[]{:S(2)}, u32[]{:S(2)}) collective-permute-start(f32[320,192]{0,1:T(8,128)S(1)} %get-tuple-element.34), channel_id=1, source_target_pairs={{0,1},{1,2},{2,3},{4,5},{5,6},{6,7},{8,9},{9,10},{10,11},{12,13},{... | collective-permute-start | bytes 737288 | tf_op jit(solution)/shard_map/ppermute | solution.py:16
  184.8 14.8 %collective-permute-start.15 = (f32[320,192]{0,1:T(8,128)S(1)}, f32[320,192]{0,1:T(8,128)S(1)}, u32[]{:S(2)}, u32[]{:S(2)}) collective-permute-start(f32[320,192]{0,1:T(8,128)S(1)} %get-tuple-element.35), channel_id=1, source_target_pairs={{1,0},{2,1},{3,2},{5,4},{6,5},{7,6},{9,8},{10,9},{11,10},{13,12},{... | collective-permute-start | bytes 737288 | tf_op jit(solution)/shard_map/ppermute | solution.py:16
  186.1 13.5 %collective-permute-start.13 = (f32[320,192]{0,1:T(8,128)S(1)}, f32[320,192]{0,1:T(8,128)S(1)}, u32[]{:S(2)}, u32[]{:S(2)}) collective-permute-start(f32[320,192]{0,1:T(8,128)S(1)} %get-tuple-element.36), channel_id=1, source_target_pairs={{4,0},{8,4},{12,8},{16,12},{20,16},{24,20},{28,24},{5,1},{9,5},{13... | collective-permute-start | bytes 737288 | tf_op jit(solution)/shard_map/ppermute | solution.py:16
  199.7 1.0 copy-start.4
  199.7 1.0 copy-start.6
  199.8 1.0 copy-start.8
  199.8 1.0 copy-start.10
  201.8 11.7 %collective-permute-start.16 = (f32[320,192]{0,1:T(8,128)}, f32[320,192]{0,1:T(8,128)}, u32[]{:S(2)}, u32[]{:S(2)}) collective-permute-start(f32[320,192]{0,1:T(8,128)} %get-tuple-element.24), channel_id=1, source_target_pairs={{0,4},{4,8},{8,12},{12,16},{16,20},{20,24},{24,28},{1,5},{5,9},{9,... | collective-permute-start | bytes 737288 | tf_op jit(solution)/shard_map/ppermute | solution.py:16
  203.8 11.4 %collective-permute-start.18 = (f32[320,192]{0,1:T(8,128)}, f32[320,192]{0,1:T(8,128)}, u32[]{:S(2)}, u32[]{:S(2)}) collective-permute-start(f32[320,192]{0,1:T(8,128)} %get-tuple-element.25), channel_id=1, source_target_pairs={{0,1},{1,2},{2,3},{4,5},{5,6},{6,7},{8,9},{9,10},{10,11},{12,13},{... | collective-permute-start | bytes 737288 | tf_op jit(solution)/shard_map/ppermute | solution.py:16
  208.3 13.5 %collective-permute-start.19 = (f32[320,192]{0,1:T(8,128)}, f32[320,192]{0,1:T(8,128)}, u32[]{:S(2)}, u32[]{:S(2)}) collective-permute-start(f32[320,192]{0,1:T(8,128)} %get-tuple-element.26), channel_id=1, source_target_pairs={{1,0},{2,1},{3,2},{5,4},{6,5},{7,6},{9,8},{10,9},{11,10},{13,12},{... | collective-permute-start | bytes 737288 | tf_op jit(solution)/shard_map/ppermute | solution.py:16
  209.5 12.2 %collective-permute-start.17 = (f32[320,192]{0,1:T(8,128)}, f32[320,192]{0,1:T(8,128)}, u32[]{:S(2)}, u32[]{:S(2)}) collective-permute-start(f32[320,192]{0,1:T(8,128)} %get-tuple-element.27), channel_id=1, source_target_pairs={{4,0},{8,4},{12,8},{16,12},{20,16},{24,20},{28,24},{5,1},{9,5},{13... | collective-permute-start | bytes 737288 | tf_op jit(solution)/shard_map/ppermute | solution.py:16
  213.4 9.7 %copy-start.5 = (f32[320,1,192]{0,2,1:T(8,128)S(1)}, f32[320,1,192]{0,2,1:T(8,128)}, u32[]{:S(2)}) copy-start(f32[320,1,192]{0,2,1:T(8,128)} %copy-done.4) | copy-start | bytes 737284
  213.4 9.7 %copy-start.7 = (f32[320,1,192]{0,2,1:T(8,128)S(1)}, f32[320,1,192]{0,2,1:T(8,128)}, u32[]{:S(2)}) copy-start(f32[320,1,192]{0,2,1:T(8,128)} %copy-done.6) | copy-start | bytes 737284
  213.4 9.7 %copy-start.9 = (f32[320,1,192]{0,2,1:T(8,128)S(1)}, f32[320,1,192]{0,2,1:T(8,128)}, u32[]{:S(2)}) copy-start(f32[320,1,192]{0,2,1:T(8,128)} %copy-done.8) | copy-start | bytes 737284
  213.4 9.7 %copy-start.11 = (f32[320,1,192]{0,2,1:T(8,128)S(1)}, f32[320,1,192]{0,2,1:T(8,128)}, u32[]{:S(2)}) copy-start(f32[320,1,192]{0,2,1:T(8,128)} %copy-done.10) | copy-start | bytes 737284
  213.4 9.7 %copy-start.39 = (f32[4]{0:T(128)S(1)}, f32[4]{0:T(128)}, u32[]{:S(2)}) copy-start(f32[4]{0:T(128)} %copy-done.37) | copy-start | bytes 52
  223.6 39.9 %copy-start.41 = (f32[320]{0:T(512)S(1)}, f32[320]{0:T(512)}, u32[]{:S(2)}) copy-start(f32[320]{0:T(512)} %copy-done.40) | copy-start | bytes 3844
  223.6 39.8 %copy-start.43 = (f32[320]{0:T(512)S(1)}, f32[320]{0:T(512)}, u32[]{:S(2)}) copy-start(f32[320]{0:T(512)} %copy-done.42) | copy-start | bytes 3844
  223.6 39.9 %copy-start.3 = (f32[1,1,320,768]{3,2,1,0:T(8,128)S(1)}, f32[1,1,320,768]{3,2,1,0:T(8,128)}, u32[]{:S(2)}) copy-start(f32[1,1,320,768]{3,2,1,0:T(8,128)} %copy.29) | copy-start | bytes 2949124
  223.6 39.9 %copy-start.36 = (f32[320]{0:T(512)S(1)}, f32[320]{0:T(512)}, u32[]{:S(2)}) copy-start(f32[320]{0:T(512)} %copy-done.35) | copy-start | bytes 3844
  (3 other events, 1.8 us)
where the time goes:
time: 267 us; the launch traced here: 266 us
  blocking collectives  137 us (51%)
  waiting for transfers between devices  43.7 us (16%)
  starting transfers between devices  39.7 us (15%)
  local copies, waits for them, and re-layouts  16.6 us (6%)
  matrix products  15.7 us (6%)
  other arithmetic  11.6 us (4%)
    psum x2, blocking collectives, paired(): return lax.psum((inner(resid, zvec), inner(zvec, wvec)), ('gx', 'gy'))  77.9 us
    ppermute x20, waiting for transfers between devices, from_behind(): lax.ppermute(value, axis, [(source, source + steps) for source in range(f...  43.7 us
    ppermute x20, starting transfers between devices, from_behind(): lax.ppermute(value, axis, [(source, source + steps) for source in range(f...  39.7 us
    all_gather x2, blocking collectives, precondition(): everyone = lax.all_gather(summed, 'gx', axis=1, tiled=True)  28.5 us
    all_gather x2, blocking collectives, precondition(): grouped = lax.all_gather(primal, 'gy', axis=1, tiled=True)  18.1 us
    unnamed x1, blocking collectives  12.4 us
    dot_general x6, matrix products, contract_last(): lax.dot_general(left, right, (((1,), (1,)), ((), ())), preferred_element_...  6.75 us
  transfers between devices with their start and end apart: 20, of which 8 were waited for; matrix products, arithmetic and copies ran while one was open for 2% of the time, Pallas kernels for 0%

commit v1 on v0

v1 whole, which is shorter than its diff:
```python
import functools

import jax
import jax.numpy as jnp
from jax import lax
from jax.experimental import pallas as pl
from jax.experimental.pallas import tpu as pltpu
from jax.sharding import PartitionSpec as P

NAGG = 2
CHUNKS = 1
HIGH = lax.Precision.HIGHEST
MESH = pl.DeviceIdType.MESH
F32 = jnp.float32
BF16 = jnp.bfloat16
NEAR = (("gx", -1), ("gx", 1), ("gy", -1), ("gy", 1))


def dot(left, right, dims, precision=None):
    return lax.dot_general(
        left, right, (dims, ((), ())), precision=precision, preferred_element_type=F32
    )


NT = ((1,), (1,))
NN = ((1,), (0,))
TN = ((0,), (0,))


def kernel(
    ngx, ngy, rows, total, prim,
    load_h, stiff_h, inv_h, phi_r, l2_r, l3_r, agg_r,
    out_h,
    load_v, stiff_v, inv_v, out_v, in_sem, out_sem,
    es, er, es_sem, er_sem,
    ps, pr, ps_sem, pr_sem, pbig,
    cg, cg_ss, cg_rs, eg, eg_ss, eg_rs, xs, xr, xs_sem, xr_sem,
    x2s, t3s,
    sa, sa_ss, sa_rs, sb, sb_ss, sb_rs,
    rr, ur, z0r, z1r, y0r, gp, cown, xown, tot,
):
    width = total // 4
    R = rows // CHUNKS
    block = NAGG * prim
    col = lax.axis_index("gx")
    row = lax.axis_index("gy")
    exists = (col > 0, col < ngx - 1, row > 0, row < ngy - 1)

    def near(e):
        axis, step = NEAR[e]
        return {axis: (col if axis == "gx" else row) + step}

    def load_copy(k):
        return pltpu.make_async_copy(
            load_h.at[0, 0, pl.ds(k * R, R)], load_v.at[pl.ds(k * R, R)], in_sem.at[2 + k]
        )

    for k in range(CHUNKS):
        load_copy(k).start()
    inv_copy = pltpu.make_async_copy(inv_h.at[0, 0], inv_v, in_sem.at[0])
    stiff_copy = pltpu.make_async_copy(stiff_h.at[0, 0], stiff_v, in_sem.at[1])
    inv_copy.start()
    stiff_copy.start()

    for e in range(4):
        @pl.when(jnp.logical_not(exists[e]))
        def _():
            er[:, :, e] = jnp.zeros((4, CHUNKS) + er.shape[3:], BF16)
            pr[e] = jnp.zeros(pr.shape[1:], F32)
            if e < 2:
                xr[:, :, e] = jnp.zeros((2, CHUNKS) + xr.shape[3:], F32)

    barrier = pltpu.get_barrier_semaphore()
    for d in range(1, ngx):
        pl.semaphore_signal(barrier, inc=1, device_id={"gx": lax.rem(col + d, ngx)}, device_id_type=MESH)
    for d in range(1, ngy):
        pl.semaphore_signal(barrier, inc=1, device_id={"gy": lax.rem(row + d, ngy)}, device_id_type=MESH)

    lane = lax.broadcasted_iota(jnp.int32, (1, total), 1)
    ew = [jnp.where(x, 0.5, 1.0).astype(F32) for x in exists]
    wrow = jnp.where(
        lane < 2 * width,
        jnp.where(lane < width, ew[0], ew[1]),
        jnp.where(lane < 3 * width, ew[2], ew[3]),
    )
    bases = (0, 128, 384, 512)
    lane128 = lax.broadcasted_iota(jnp.int32, (1, 128), 1)
    low = lane128 < 64
    low192 = lax.broadcasted_iota(jnp.int32, (1, 256), 1) < 192

    def aligned(x, e):
        part = x[:, bases[e]:bases[e] + 256]
        return pltpu.roll(part, 192, 1) if e % 2 else part

    def put_back(part, e):
        part = jnp.where(low192, part, 0.0)
        return pltpu.roll(part, 64, 1) if e % 2 else part

    def pack(x, e):
        a = aligned(x, e)
        first, second = a[:, :128], a[:, 128:]
        return first, jnp.where(low, second[: R // 2], pltpu.roll(second[R // 2:], 64, 1))

    def edge_copy(x, k, e):
        return pltpu.make_async_remote_copy(
            src_ref=es.at[x, k, e], dst_ref=er.at[x, k, e ^ 1],
            send_sem=es_sem.at[x, k, e], recv_sem=er_sem.at[x, k, e ^ 1],
            device_id=near(e), device_id_type=MESH,
        )

    def edge_wait(x, k, e):
        return pltpu.make_async_remote_copy(
            src_ref=es.at[x, k, e], dst_ref=er.at[x, k, e],
            send_sem=es_sem.at[x, k, e], recv_sem=er_sem.at[x, k, e],
            device_id=near(e), device_id_type=MESH,
        )

    def send_edges(x, k, value):
        for e in (2, 3, 0, 1):
            a, b = pack(value, e)
            es[x, k, e, :R] = a.astype(BF16)
            es[x, k, e, R:] = b.astype(BF16)

            @pl.when(exists[e])
            def _():
                edge_copy(x, k, e).start()

    def wait_edges(x, k):
        for e in (0, 1, 2, 3):
            @pl.when(exists[e])
            def _():
                edge_wait(x, k, e).wait_recv()

    def with_edges(x, k, value):
        added = []
        for e in range(4):
            a = er[x, k, e, :R].astype(F32)
            b = er[x, k, e, R:].astype(F32)
            b = jnp.concatenate([b, pltpu.roll(b, 64, 1)], axis=0)
            added.append(put_back(jnp.concatenate([a, b], axis=1), e))
        parts = []
        for s in range(2):
            first, second = added[2 * s], added[2 * s + 1]
            parts += [first[:, :128], first[:, 128:] + second[:, :128], second[:, 128:]]
        return value + jnp.concatenate(parts, axis=1)

    phi = phi_r[0, 0]
    phi_hi = phi.astype(BF16)
    phi_lo = (phi - phi_hi.astype(F32)).astype(BF16)
    phi2 = jnp.concatenate([phi_hi, phi_lo], axis=0)
    masks = [jnp.where(agg_r[0, 0] == q, 1.0, 0.0).astype(F32) for q in range(NAGG)]
    pown = jnp.concatenate([phi] + [phi * m for m in masks], axis=0) * wrow
    prow = pown.shape[0]
    pbig[...] = jnp.zeros_like(pbig)
    pbig[0:prow, :] = pown
    for e in range(4):
        ps[e] = aligned(pown, e)

    def base_copy(e, there):
        return pltpu.make_async_remote_copy(
            src_ref=ps.at[e], dst_ref=pr.at[there], send_sem=ps_sem.at[e], recv_sem=pr_sem.at[there],
            device_id=near(e), device_id_type=MESH,
        )

    pl.semaphore_wait(barrier, ngx - 1 + ngy - 1)

    def spread(buf, ssem, rsem, t, k, axis):
        me, n = (col, ngx) if axis == "gx" else (row, ngy)
        for d in range(1, n):
            pltpu.make_async_remote_copy(
                src_ref=buf.at[t, k, me], dst_ref=buf.at[t, k, me],
                send_sem=ssem.at[t, k, d], recv_sem=rsem.at[t, k, me],
                device_id={axis: lax.rem(me + d, n)}, device_id_type=MESH,
            ).start()

    def gathered(buf, ssem, rsem, t, k, axis):
        me, n = (col, ngx) if axis == "gx" else (row, ngy)
        for d in range(1, n):
            src = lax.rem(me + d, n)
            pltpu.make_async_remote_copy(
                src_ref=buf.at[t, k, src], dst_ref=buf.at[t, k, src],
                send_sem=ssem.at[t, k, d], recv_sem=rsem.at[t, k, src],
                device_id={axis: src}, device_id_type=MESH,
            ).wait_recv()

    def sent(buf, ssem, rsem, t, k, axis):
        me, n = (col, ngx) if axis == "gx" else (row, ngy)
        for d in range(1, n):
            pltpu.make_async_remote_copy(
                src_ref=buf.at[t, k, me], dst_ref=buf.at[t, k, me],
                send_sem=ssem.at[t, k, d], recv_sem=rsem.at[t, k, me],
                device_id={axis: lax.rem(me + d, n)}, device_id_type=MESH,
            ).wait_send()

    def x_copy(t, k, e, there):
        return pltpu.make_async_remote_copy(
            src_ref=xs.at[t, k], dst_ref=xr.at[t, k, there],
            send_sem=xs_sem.at[t, k, e], recv_sem=xr_sem.at[t, k, there],
            device_id=near(e), device_id_type=MESH,
        )

    def fold(v):
        acc = v[:, :128]
        for i in range(128, total, 128):
            acc = acc + v[:, i:i + 128]
        return acc

    def rows_of(parts):
        line = lax.broadcasted_iota(jnp.int32, (8, 128), 0)
        out = None
        for q, part in parts:
            one = dot(jnp.where(line == q, 1.0, 0.0).astype(F32), part, NT, HIGH)
            out = one if out is None else out + one
        return out

    def columns_of(values):
        n = len(values)
        line8 = lax.broadcasted_iota(jnp.int32, (8, R), 0)
        v = jnp.zeros((8, R), F32)
        for q, val in enumerate(values):
            v = jnp.where(line8 == q, val, v)
        line = lax.broadcasted_iota(jnp.int32, (8, 128 * n), 0)
        lanes = lax.broadcasted_iota(jnp.int32, (8, 128 * n), 1)
        pick = jnp.where((lanes >= line * 128) & (lanes < line * 128 + 128), 1.0, 0.0).astype(F32)
        c = dot(v, pick, TN, HIGH)
        return [c[:, 128 * q:128 * q + 128] for q in range(n)]

    def wide(c):
        return jnp.concatenate([c] * (total // 128), axis=1)

    def start(k):
        load_copy(k).wait()
        send_edges(0, k, load_v[pl.ds(k * R, R), :])

    def local_part(t, k, r):
        rs = wrow * r
        rsb = rs.astype(BF16)
        c = dot(phi2, rsb, NT)
        c = c[:prim] + c[prim:]
        cown[t, k] = c
        cg[t, k, row] = jnp.concatenate([c * m for m in masks], axis=0)
        spread(cg, cg_ss, cg_rs, t, k, "gy")
        if t == 0 and k == 0:
            inv_copy.wait()
        local = dot(rsb, inv_v[...], NN)
        u = wrow * local
        send_edges(1 + 2 * t, k, u)
        ur[t, k] = u
        gp[t, k] = fold(r * u)

    def first_local(k):
        wait_edges(0, k)
        r = with_edges(0, k, load_v[pl.ds(k * R, R), :])
        rr[k] = r
        local_part(0, k, r)

    def middle(t, k):
        gathered(cg, cg_ss, cg_rs, t, k, "gy")
        e = cg[t, k, 0]
        cs = [e[:prim] + e[prim:]]
        for j in range(1, ngy):
            o = cg[t, k, j]
            cs.append(o[:prim] + o[prim:])
            e = e + o
        eg[t, k, col] = e.astype(BF16)
        spread(eg, eg_ss, eg_rs, t, k, "gx")
        x2s[...] = dot(l2_r[0], jnp.concatenate(cs, axis=0), NN, HIGH)
        x2 = x2s[pl.ds(pl.multiple_of(row * prim, prim), prim), :]
        xs[t, k] = x2
        for e_ in range(2):
            @pl.when(exists[e_])
            def _():
                x_copy(t, k, e_, e_ ^ 1).start()
        before = x2s[pl.ds(pl.multiple_of(jnp.maximum(row - 1, 0) * prim, prim), prim), :]
        after = x2s[pl.ds(pl.multiple_of(jnp.minimum(row + 1, ngy - 1) * prim, prim), prim), :]
        xown[t, k, 0] = x2
        xown[t, k, 1] = before
        xown[t, k, 2] = after

    def direction(t, k):
        gathered(eg, eg_ss, eg_rs, t, k, "gx")
        e = jnp.concatenate([eg[t, k, i] for i in range(ngx)], axis=0)
        t3s[...] = dot(l3_r[...], e, NN)

        def t3(i):
            return t3s[pl.ds(pl.multiple_of(i * block, block), block), :]

        here, behind, ahead = t3(col), t3(jnp.maximum(col - 1, 0)), t3(jnp.minimum(col + 1, ngx - 1))
        for e_ in range(2):
            @pl.when(exists[e_])
            def _():
                x_copy(t, k, e_, e_).wait_recv()
        if t == 0 and k == 0:
            for e_ in range(4):
                @pl.when(exists[e_])
                def _():
                    base_copy(e_, e_).wait_recv()
                at = prow * (1 + e_)
                base = bases[e_]
                pbig[at:at + prow, base:base + 256] = put_back(pr[e_], e_)
        own = xown[t, k, 0]
        x = jnp.concatenate(
            [own, here, xr[t, k, 0], behind, xr[t, k, 1], ahead, xown[t, k, 1], here, xown[t, k, 2], here], axis=0
        )
        coarse = dot(x, pbig[...], TN, HIGH)
        full = own
        for q, m in enumerate(masks):
            full = full + m * here[q * prim:(q + 1) * prim]
        extra = jnp.sum(cown[t, k] * full, axis=0, keepdims=True)
        wait_edges(1 + 2 * t, k)
        z = with_edges(1 + 2 * t, k, ur[t, k] + coarse)
        return z, extra

    def message(t, k, parts, extra):
        m = rows_of(parts)
        line8 = lax.broadcasted_iota(jnp.int32, (8, R), 0)
        sa[t, k, row] = m + jnp.where(line8 == 0, extra, 0.0)
        spread(sa, sa_ss, sa_rs, t, k, "gy")

    def first_apply(k):
        z, extra = direction(0, k)
        if k == 0:
            stiff_copy.wait()
        y = dot(z.astype(BF16), stiff_v[...], NN)
        send_edges(2, k, y)
        message(0, k, [(0, gp[0, k]), (1, fold(z * y))], extra)
        z0r[k] = z
        y0r[k] = y

    def second_apply(k):
        z, extra = direction(1, k)
        y = dot(z.astype(BF16), stiff_v[...], NN)
        message(1, k, [(0, gp[1, k]), (1, fold(z * y)), (2, fold(z * y0r[k] + z0r[k] * y))], extra)
        z1r[k] = z

    def relay(t, k):
        gathered(sa, sa_ss, sa_rs, t, k, "gy")
        s = sa[t, k, 0]
        for j in range(1, ngy):
            s = s + sa[t, k, j]
        sb[t, k, col] = s
        spread(sb, sb_ss, sb_rs, t, k, "gx")

    def summed(t, k):
        gathered(sb, sb_ss, sb_rs, t, k, "gx")
        s = sb[t, k, 0]
        for j in range(1, ngx):
            s = s + sb[t, k, j]
        return s

    def second_local(k):
        s = summed(0, k)
        tot[k] = s
        alpha, = columns_of([s[0:1] / s[1:2]])
        wait_edges(2, k)
        r = rr[k] - wide(alpha) * with_edges(2, k, y0r[k])
        local_part(1, k, r)

    def out_copy(k):
        return pltpu.make_async_copy(out_v.at[pl.ds(k * R, R)], out_h.at[0, 0, pl.ds(k * R, R)], out_sem.at[k])

    def finish(k):
        s0, s1 = tot[k], summed(1, k)
        gamma, delta = s0[0:1], s0[1:2]
        new = s1[0:1]
        beta = new / gamma
        alpha1 = new / (s1[1:2] + beta * s1[2:3] + beta * beta * delta)
        first, second = columns_of([gamma / delta + alpha1 * beta, alpha1])
        out_v[pl.ds(k * R, R), :] = wide(first) * z0r[k] + wide(second) * z1r[k]
        out_copy(k).start()

    steps = [
        start, first_local, functools.partial(middle, 0), first_apply, functools.partial(relay, 0),
        second_local, functools.partial(middle, 1), second_apply, functools.partial(relay, 1), finish,
    ]
    for index, step in enumerate(steps):
        for k in range(CHUNKS):
            step(k)
        if index == 0:
            for e in range(4):
                @pl.when(exists[e])
                def _():
                    base_copy(e, e ^ 1).start()

    for k in range(CHUNKS):
        out_copy(k).wait()
        for e in range(4):
            @pl.when(exists[e])
            def _():
                for x in range(4):
                    edge_copy(x, k, e).wait_send()
                if k == 0:
                    base_copy(e, e ^ 1).wait_send()
                if e < 2:
                    for t in range(2):
                        x_copy(t, k, e, e ^ 1).wait_send()
        for t in range(2):
            sent(cg, cg_ss, cg_rs, t, k, "gy")
            sent(eg, eg_ss, eg_rs, t, k, "gx")
            sent(sa, sa_ss, sa_rs, t, k, "gy")
            sent(sb, sb_ss, sb_rs, t, k, "gx")


def body(load, stiffness, local_inverse, phi, level2_inverse, level3_inverse, aggregate):
    rows, total = load.shape[2:]
    prim = phi.shape[2]
    ngx, ngy = lax.axis_size("gx"), lax.axis_size("gy")
    R, C, block = rows // CHUNKS, CHUNKS, NAGG * prim
    prow = prim + block
    dma = pltpu.SemaphoreType.DMA
    vmem = pltpu.VMEM
    anyw = pl.BlockSpec(memory_space=pl.ANY)
    here = pl.BlockSpec(memory_space=pltpu.VMEM)
    scratch = [
        vmem((rows, total), F32), vmem((total, total), BF16), vmem((total, total), BF16), vmem((rows, total), F32),
        dma((2 + C,)), dma((C,)),
        vmem((4, C, 4, R + R // 2, 128), BF16), vmem((4, C, 4, R + R // 2, 128), BF16), dma((4, C, 4)), dma((4, C, 4)),
        vmem((4, prow, 256), F32), vmem((4, prow, 256), F32), dma((4,)), dma((4,)), vmem((5 * prow, total), F32),
        vmem((2, C, ngy, block, R), F32), dma((2, C, ngy)), dma((2, C, ngy)),
        vmem((2, C, ngx, block, R), BF16), dma((2, C, ngx)), dma((2, C, ngx)),
        vmem((2, C, prim, R), F32), vmem((2, C, 2, prim, R), F32), dma((2, C, 2)), dma((2, C, 2)),
        vmem((ngy * prim, R), F32), vmem((ngx * block, R), F32),
        vmem((2, C, ngy, 8, R), F32), dma((2, C, ngy)), dma((2, C, ngy)),
        vmem((2, C, ngx, 8, R), F32), dma((2, C, ngx)), dma((2, C, ngx)),
        vmem((C, R, total), F32), vmem((2, C, R, total), F32), vmem((C, R, total), F32), vmem((C, R, total), F32),
        vmem((C, R, total), F32), vmem((2, C, R, 128), F32), vmem((2, C, prim, R), F32), vmem((2, C, 3, prim, R), F32),
        vmem((C, 8, R), F32),
    ]
    return pl.pallas_call(
        functools.partial(kernel, ngx, ngy, rows, total, prim),
        out_shape=jax.ShapeDtypeStruct((1, 1, rows, total), F32),
        in_specs=[anyw, anyw, anyw, here, here, here, pl.BlockSpec(memory_space=pltpu.SMEM)],
        out_specs=anyw,
        scratch_shapes=scratch,
        compiler_params=pltpu.CompilerParams(
            collective_id=0, has_side_effects=True, vmem_limit_bytes=60 * 1024 * 1024
        ),
    )(load, stiffness, local_inverse, phi, level2_inverse, level3_inverse, aggregate)


def solution(mesh):
    return jax.shard_map(
        body,
        mesh=mesh,
        in_specs=(
            P("gx", "gy", None, None),
            P("gx", "gy", None, None),
            P("gx", "gy", None, None),
            P("gx", "gy", None, None),
            P("gx", None, None),
            P(),
            P("gx", "gy"),
        ),
        out_specs=P("gx", "gy", None, None),
        check_vma=False,
    )
```

time: 267 us -> 62 us (0.23)
  blocking collectives: 137 us -> 0 us
  Pallas kernels: 0 us -> 58.9 us
  waiting for transfers between devices: 43.7 us -> 0 us
  starting transfers between devices: 39.7 us -> 0 us
  matrix products: 15.7 us -> 0 us
  local copies, waits for them, and re-layouts: 16.6 us -> 2.21 us
  other arithmetic: 11.6 us -> 0 us
    psum x2 -> x0, blocking collectives: 77.9 us -> none  [paired(): return lax.psum((inner(resid, zvec), inner(zvec, wvec)), ('gx', 'gy'))]
    pallas_call x0 -> x1, Pallas kernels: none -> 58.9 us  [body(): pl.pallas_call(functools.partial(kernel, ngx, ngy, rows, total, prim), ou...]
    all_gather x4 -> x0, blocking collectives: 46.7 us -> none  [the longest x2 28.5 us: precondition(): everyone = lax.all_gather(summed, 'gx', axis=1, tiled=True)]
    ppermute x20 -> x0, waiting for transfers between devices: 43.7 us -> none  [from_behind(): lax.ppermute(value, axis, [(source, source + steps) for source in range(f...]
    ppermute x20 -> x0, starting transfers between devices: 39.7 us -> none  [from_behind(): lax.ppermute(value, axis, [(source, source + steps) for source in range(f...]
    dot_general x16 -> x0, matrix products: 15.7 us -> none  [the longest x6 6.75 us: contract_last(): lax.dot_general(left, right, (((1,), (1,)), ((), ())), preferred_element_...]
    unnamed x1 -> x0, blocking collectives: 12.4 us -> none
    reshape x2 -> x0, local copies, waits for them, and re-layouts: 3.89 us -> none  [assemble(): jnp.stack([new_west, new_east, new_south, new_north], axis=1)]
  transfers between devices with their start and end apart: 20 -> 0, of which waited for: 8 -> 0; matrix products, arithmetic and copies ran while one was open for 2% -> 0% of each run, Pallas kernels for 0% -> 0%
where the time goes in v1:
time: 62 us; the launch traced here: 61.8 us
  Pallas kernels  58.9 us (95%)
  local copies, waits for them, and re-layouts  2.21 us (4%)
  between operations  0.66 us (1%)
    pallas_call x1, Pallas kernels, body(): pl.pallas_call(functools.partial(kernel, ngx, ngy, rows, total, prim), ou...  58.9 us
    unnamed x1, local copies, waits for them, and re-layouts  2.21 us

profile of v1, /device:TPU:0, one launch (start us, length us, event | category | flops | bytes accessed | tf_op | source)
XLA Modules:
  0.0 61.8 jit_solution(15987025584695359137)
XLA Ops:
  0.7 58.9 %shard_map.73 = f32[1,1,320,768]{3,2,1,0:T(8,128)} custom-call(f32[1,1,320,768]{3,2,1,0:T(8,128)} %load_h.1, bf16[1,1,768,768]{3,2,1,0:T(8,128)(2,1)} %stiff_h.1, bf16[1,1,768,768]{3,2,1,0:T(8,128)(2,1)} %inv_h.1, f32[1,1,8,768]{3,2,1,0:T(8,128)} %phi_r.1, f32[1,32,32]{2,1,0:T(8,128)} %l2_r.1, bf16[128,128]{1,0:T(8,128)(2,1)} %l3_r.1, s32[1,1]{1,0:T(1,128)S(6)} %copy.9.agg_r), custom_call_target="tpu_custom_call" | custom-call | tf_op jit(solution)/shard_map/pallas_call | solution.py:429
  59.6 2.2 %copy.10 = f32[1,1,320,768]{3,2,1,0:T(8,128)} copy(f32[1,1,320,768]{3,2,1,0:T(8,128)} %shard_map.73) | data formatting | bytes 1966080

commit v2 on v1

--- a/solution.py
+++ b/solution.py
@@ -33,11 +33,12 @@
     out_h,
     load_v, stiff_v, inv_v, out_v, in_sem, out_sem,
     es, er, es_sem, er_sem,
-    ps, pr, ps_sem, pr_sem, pbig,
+    ps, pr, ps_sem, pr_sem, pbig, pbigb, pplain,
+    ns, nr, ns_sem, nr_sem,
     cg, cg_ss, cg_rs, eg, eg_ss, eg_rs, xs, xr, xs_sem, xr_sem,
     x2s, t3s,
     sa, sa_ss, sa_rs, sb, sb_ss, sb_rs,
-    rr, ur, z0r, z1r, y0r, gp, cown, xown, tot,
+    rr, ur, z0r, z1r, y0r, gp, cown, xown, xall, xfull, tot,
 ):
     width = total // 4
     R = rows // CHUNKS
@@ -67,6 +68,7 @@
         def _():
             er[:, :, e] = jnp.zeros((4, CHUNKS) + er.shape[3:], BF16)
             pr[e] = jnp.zeros(pr.shape[1:], F32)
+            nr[:, e] = jnp.zeros((CHUNKS,) + nr.shape[2:], F32)
             if e < 2:
                 xr[:, :, e] = jnp.zeros((2, CHUNKS) + xr.shape[3:], F32)
 
@@ -163,6 +165,10 @@
         )
 
     pl.semaphore_wait(barrier, ngx - 1 + ngy - 1)
+    for e in range(4):
+        @pl.when(exists[e])
+        def _():
+            base_copy(e, e ^ 1).start()
 
     def spread(buf, ssem, rsem, t, k, axis):
         me, n = (col, ngx) if axis == "gx" else (row, ngy)
@@ -205,24 +211,43 @@
             acc = acc + v[:, i:i + 128]
         return acc
 
-    def rows_of(parts):
-        line = lax.broadcasted_iota(jnp.int32, (8, 128), 0)
-        out = None
-        for q, part in parts:
-            one = dot(jnp.where(line == q, 1.0, 0.0).astype(F32), part, NT, HIGH)
-            out = one if out is None else out + one
+    def halves(v, axis):
+        hi = v.astype(BF16)
+        return jnp.concatenate([hi, (v - hi.astype(F32)).astype(BF16)], axis=axis)
+
+    line8 = lax.broadcasted_iota(jnp.int32, (8, 128), 0)
+
+    def tile_of(parts, extra):
+        v = halves(jnp.concatenate(parts, axis=0), 1)
+        line = lax.broadcasted_iota(jnp.int32, (8, 256), 0)
+        out = jnp.zeros((8, 128), F32)
+        for m in range(-(-v.shape[0] // 128)):
+            piece = v[m * 128:(m + 1) * 128]
+            if piece.shape[0] < 128:
+                piece = jnp.concatenate([piece, jnp.zeros((128 - piece.shape[0], 256), BF16)], axis=0)
+            out = out + dot(jnp.where(line == m, 1.0, 0.0).astype(BF16), piece, NT)
+        pad = -(-R // 128) * 128
+        if pad > R:
+            extra = jnp.concatenate([extra, jnp.zeros((1, pad - R), F32)], axis=1)
+        for m in range(pad // 128):
+            out = out + jnp.where(line8 == m, extra[:, m * 128:(m + 1) * 128], 0.0)
         return out
+
+    def rows_from(tile, count):
+        flat = jnp.concatenate([tile[m:m + 1] for m in range(8)], axis=1)
+        return [(flat if q == 0 else pltpu.roll(flat, 1024 - q * R, 1))[:, :R] for q in range(count)]
 
     def columns_of(values):
         n = len(values)
-        line8 = lax.broadcasted_iota(jnp.int32, (8, R), 0)
+        place = lax.broadcasted_iota(jnp.int32, (8, R), 0)
         v = jnp.zeros((8, R), F32)
         for q, val in enumerate(values):
-            v = jnp.where(line8 == q, val, v)
-        line = lax.broadcasted_iota(jnp.int32, (8, 128 * n), 0)
-        lanes = lax.broadcasted_iota(jnp.int32, (8, 128 * n), 1)
-        pick = jnp.where((lanes >= line * 128) & (lanes < line * 128 + 128), 1.0, 0.0).astype(F32)
-        c = dot(v, pick, TN, HIGH)
+            v = jnp.where(place == q, val, v)
+        v = halves(v, 0)
+        line = lax.broadcasted_iota(jnp.int32, (16, 128 * n), 0) % 8
+        lanes = lax.broadcasted_iota(jnp.int32, (16, 128 * n), 1)
+        pick = jnp.where((lanes >= line * 128) & (lanes < line * 128 + 128), 1.0, 0.0).astype(BF16)
+        c = dot(v, pick, TN)
         return [c[:, 128 * q:128 * q + 128] for q in range(n)]
 
     def wide(c):
@@ -232,18 +257,13 @@
         load_copy(k).wait()
         send_edges(0, k, load_v[pl.ds(k * R, R), :])
 
-    def local_part(t, k, r):
-        rs = wrow * r
-        rsb = rs.astype(BF16)
-        c = dot(phi2, rsb, NT)
-        c = c[:prim] + c[prim:]
+    def solve_coarse(t, k, c):
         cown[t, k] = c
         cg[t, k, row] = jnp.concatenate([c * m for m in masks], axis=0)
         spread(cg, cg_ss, cg_rs, t, k, "gy")
-        if t == 0 and k == 0:
-            inv_copy.wait()
-        local = dot(rsb, inv_v[...], NN)
-        u = wrow * local
+
+    def local_part(t, k, r, rsb):
+        u = wrow * dot(rsb, inv_v[...], NN)
         send_edges(1 + 2 * t, k, u)
         ur[t, k] = u
         gp[t, k] = fold(r * u)
@@ -251,8 +271,13 @@
     def first_local(k):
         wait_edges(0, k)
         r = with_edges(0, k, load_v[pl.ds(k * R, R), :])
+        rsb = (wrow * r).astype(BF16)
+        c = dot(phi2, rsb, NT)
+        solve_coarse(0, k, c[:prim] + c[prim:])
         rr[k] = r
-        local_part(0, k, r)
+        if k == 0:
+            inv_copy.wait()
+        local_part(0, k, r, rsb)
 
     def middle(t, k):
         gathered(cg, cg_ss, cg_rs, t, k, "gy")
@@ -277,6 +302,17 @@
         xown[t, k, 1] = before
         xown[t, k, 2] = after
 
+    def bases_here():
+        for e_ in range(4):
+            @pl.when(exists[e_])
+            def _():
+                base_copy(e_, e_).wait_recv()
+            at = prow * (1 + e_)
+            base = bases[e_]
+            pbig[at:at + prow, base:base + 256] = put_back(pr[e_], e_)
+        pbigb[...] = pbig[...].astype(BF16)
+        pplain[...] = jnp.concatenate([pbig[prow * i:prow * i + prim, :] for i in range(5)], axis=0).astype(BF16)
+
     def direction(t, k):
         gathered(eg, eg_ss, eg_rs, t, k, "gx")
         e = jnp.concatenate([eg[t, k, i] for i in range(ngx)], axis=0)
@@ -290,47 +326,71 @@
             @pl.when(exists[e_])
             def _():
                 x_copy(t, k, e_, e_).wait_recv()
-        if t == 0 and k == 0:
-            for e_ in range(4):
-                @pl.when(exists[e_])
-                def _():
-                    base_copy(e_, e_).wait_recv()
-                at = prow * (1 + e_)
-                base = bases[e_]
-                pbig[at:at + prow, base:base + 256] = put_back(pr[e_], e_)
         own = xown[t, k, 0]
         x = jnp.concatenate(
             [own, here, xr[t, k, 0], behind, xr[t, k, 1], ahead, xown[t, k, 1], here, xown[t, k, 2], here], axis=0
         )
-        coarse = dot(x, pbig[...], TN, HIGH)
         full = own
         for q, m in enumerate(masks):
             full = full + m * here[q * prim:(q + 1) * prim]
-        extra = jnp.sum(cown[t, k] * full, axis=0, keepdims=True)
+        c = cown[t, k]
+        if t == 0:
+            xall[k] = x
+            xfull[k] = full
+        else:
+            alpha = tot[k, 2:3]
+            x = xall[k] - alpha * x
+            full = xfull[k] - alpha * full
+            c = cown[0, k] - alpha * c
+        coarse = dot(x.astype(BF16), pbigb[...], TN)
+        extra = jnp.sum(c * full, axis=0, keepdims=True)
         wait_edges(1 + 2 * t, k)
         z = with_edges(1 + 2 * t, k, ur[t, k] + coarse)
         return z, extra
 
     def message(t, k, parts, extra):
-        m = rows_of(parts)
-        line8 = lax.broadcasted_iota(jnp.int32, (8, R), 0)
-        sa[t, k, row] = m + jnp.where(line8 == 0, extra, 0.0)
+        sa[t, k, row] = tile_of(parts, extra)
         spread(sa, sa_ss, sa_rs, t, k, "gy")
 
+    def coarse_copy(k, e, there):
+        return pltpu.make_async_remote_copy(
+            src_ref=ns.at[k, e], dst_ref=nr.at[k, there], send_sem=ns_sem.at[k, e], recv_sem=nr_sem.at[k, there],
+            device_id=near(e), device_id_type=MESH,
+        )
+
     def first_apply(k):
+        if k == 0:
+            bases_here()
         z, extra = direction(0, k)
         if k == 0:
             stiff_copy.wait()
         y = dot(z.astype(BF16), stiff_v[...], NN)
+        y0r[k] = y
+        z0r[k] = z
+        message(0, k, [gp[0, k], fold(z * y)], extra)
+        ct = dot(pplain[...], y.astype(BF16), NT)
+        cown[1, k] = ct[:prim]
+        for e in (2, 3, 0, 1):
+            ns[k, e] = ct[prim * (1 + e):prim * (2 + e)]
+
+            @pl.when(exists[e])
+            def _():
+                coarse_copy(k, e, e ^ 1).start()
         send_edges(2, k, y)
-        message(0, k, [(0, gp[0, k]), (1, fold(z * y))], extra)
-        z0r[k] = z
-        y0r[k] = y
+
+    def coarse_start(k):
+        c = cown[1, k]
+        for e in range(4):
+            @pl.when(exists[e])
+            def _():
+                coarse_copy(k, e, e).wait_recv()
+            c = c + nr[k, e]
+        solve_coarse(1, k, c)
 
     def second_apply(k):
         z, extra = direction(1, k)
         y = dot(z.astype(BF16), stiff_v[...], NN)
-        message(1, k, [(0, gp[1, k]), (1, fold(z * y)), (2, fold(z * y0r[k] + z0r[k] * y))], extra)
+        message(1, k, [gp[1, k], fold(z * y), fold(z * y0r[k] + z0r[k] * y)], extra)
         z1r[k] = z
 
     def relay(t, k):
@@ -346,41 +406,38 @@
         s = sb[t, k, 0]
         for j in range(1, ngx):
             s = s + sb[t, k, j]
-        return s
+        return rows_from(s, 2 + t)
 
     def second_local(k):
-        s = summed(0, k)
-        tot[k] = s
-        alpha, = columns_of([s[0:1] / s[1:2]])
+        gamma, delta = summed(0, k)
+        rate = gamma / delta
+        tot[k, 0:1] = gamma
+        tot[k, 1:2] = delta
+        tot[k, 2:3] = rate
+        alpha, = columns_of([rate])
         wait_edges(2, k)
         r = rr[k] - wide(alpha) * with_edges(2, k, y0r[k])
-        local_part(1, k, r)
+        local_part(1, k, r, (wrow * r).astype(BF16))
 
     def out_copy(k):
         return pltpu.make_async_copy(out_v.at[pl.ds(k * R, R)], out_h.at[0, 0, pl.ds(k * R, R)], out_sem.at[k])
 
     def finish(k):
-        s0, s1 = tot[k], summed(1, k)
-        gamma, delta = s0[0:1], s0[1:2]
-        new = s1[0:1]
+        gamma, delta, rate = tot[k, 0:1], tot[k, 1:2], tot[k, 2:3]
+        new, along, across = summed(1, k)
         beta = new / gamma
-        alpha1 = new / (s1[1:2] + beta * s1[2:3] + beta * beta * delta)
-        first, second = columns_of([gamma / delta + alpha1 * beta, alpha1])
+        alpha1 = new / (along + beta * across + beta * beta * delta)
+        first, second = columns_of([rate + alpha1 * beta, alpha1])
         out_v[pl.ds(k * R, R), :] = wide(first) * z0r[k] + wide(second) * z1r[k]
         out_copy(k).start()
 
     steps = [
-        start, first_local, functools.partial(middle, 0), first_apply, functools.partial(relay, 0),
+        start, first_local, functools.partial(middle, 0), first_apply, functools.partial(relay, 0), coarse_start,
         second_local, functools.partial(middle, 1), second_apply, functools.partial(relay, 1), finish,
     ]
     for index, step in enumerate(steps):
         for k in range(CHUNKS):
             step(k)
-        if index == 0:
-            for e in range(4):
-                @pl.when(exists[e])
-                def _():
-                    base_copy(e, e ^ 1).start()
 
     for k in range(CHUNKS):
         out_copy(k).wait()
@@ -389,6 +446,7 @@
             def _():
                 for x in range(4):
                     edge_copy(x, k, e).wait_send()
+                coarse_copy(k, e, e ^ 1).wait_send()
                 if k == 0:
                     base_copy(e, e ^ 1).wait_send()
                 if e < 2:
@@ -416,15 +474,17 @@
         dma((2 + C,)), dma((C,)),
         vmem((4, C, 4, R + R // 2, 128), BF16), vmem((4, C, 4, R + R // 2, 128), BF16), dma((4, C, 4)), dma((4, C, 4)),
         vmem((4, prow, 256), F32), vmem((4, prow, 256), F32), dma((4,)), dma((4,)), vmem((5 * prow, total), F32),
+        vmem((5 * prow, total), BF16), vmem((5 * prim, total), BF16),
+        vmem((C, 4, prim, R), F32), vmem((C, 4, prim, R), F32), dma((C, 4)), dma((C, 4)),
         vmem((2, C, ngy, block, R), F32), dma((2, C, ngy)), dma((2, C, ngy)),
         vmem((2, C, ngx, block, R), BF16), dma((2, C, ngx)), dma((2, C, ngx)),
         vmem((2, C, prim, R), F32), vmem((2, C, 2, prim, R), F32), dma((2, C, 2)), dma((2, C, 2)),
         vmem((ngy * prim, R), F32), vmem((ngx * block, R), F32),
-        vmem((2, C, ngy, 8, R), F32), dma((2, C, ngy)), dma((2, C, ngy)),
-        vmem((2, C, ngx, 8, R), F32), dma((2, C, ngx)), dma((2, C, ngx)),
+        vmem((2, C, ngy, 8, 128), F32), dma((2, C, ngy)), dma((2, C, ngy)),
+        vmem((2, C, ngx, 8, 128), F32), dma((2, C, ngx)), dma((2, C, ngx)),
         vmem((C, R, total), F32), vmem((2, C, R, total), F32), vmem((C, R, total), F32), vmem((C, R, total), F32),
         vmem((C, R, total), F32), vmem((2, C, R, 128), F32), vmem((2, C, prim, R), F32), vmem((2, C, 3, prim, R), F32),
-        vmem((C, 8, R), F32),
+        vmem((C, 5 * prow, R), F32), vmem((C, prim, R), F32), vmem((C, 8, R), F32),
     ]
     return pl.pallas_call(
         functools.partial(kernel, ngx, ngy, rows, total, prim),

time: 62 us -> 55.5 us (0.90)
  Pallas kernels: 58.9 us -> 52.4 us
    pallas_call x1, Pallas kernels: 58.9 us -> 52.4 us  [body(): pl.pallas_call(functools.partial(kernel, ngx, ngy, rows, total, prim), ou...]
where the time goes in v2:
time: 55.5 us; the launch traced here: 55.3 us
  Pallas kernels  52.4 us (94%)
  local copies, waits for them, and re-layouts  2.21 us (4%)
  between operations  0.66 us (1%)
    pallas_call x1, Pallas kernels, body(): pl.pallas_call(functools.partial(kernel, ngx, ngy, rows, total, prim), ou...  52.4 us
    unnamed x1, local copies, waits for them, and re-layouts  2.21 us

profile of v2, /device:TPU:0, one launch (start us, length us, event | category | flops | bytes accessed | tf_op | source)
XLA Modules:
  0.0 55.3 jit_solution(11262066062667801487)
XLA Ops:
  0.7 52.4 %shard_map.73 = f32[1,1,320,768]{3,2,1,0:T(8,128)} custom-call(f32[1,1,320,768]{3,2,1,0:T(8,128)} %load_h.1, bf16[1,1,768,768]{3,2,1,0:T(8,128)(2,1)} %stiff_h.1, bf16[1,1,768,768]{3,2,1,0:T(8,128)(2,1)} %inv_h.1, f32[1,1,8,768]{3,2,1,0:T(8,128)} %phi_r.1, f32[1,32,32]{2,1,0:T(8,128)} %l2_r.1, bf16[128,128]{1,0:T(8,128)(2,1)} %l3_r.1, s32[1,1]{1,0:T(1,128)S(6)} %copy.9.agg_r), custom_call_target="tpu_custom_call" | custom-call | tf_op jit(solution)/shard_map/pallas_call | solution.py:489
  53.1 2.2 %copy.10 = f32[1,1,320,768]{3,2,1,0:T(8,128)} copy(f32[1,1,320,768]{3,2,1,0:T(8,128)} %shard_map.73) | data formatting | bytes 1966080

commit v3 on v2

--- a/solution.py
+++ b/solution.py
@@ -8,7 +8,7 @@
 from jax.sharding import PartitionSpec as P
 
 NAGG = 2
-CHUNKS = 1
+CHUNKS = 2
 HIGH = lax.Precision.HIGHEST
 MESH = pl.DeviceIdType.MESH
 F32 = jnp.float32
@@ -31,7 +31,7 @@
     ngx, ngy, rows, total, prim,
     load_h, stiff_h, inv_h, phi_r, l2_r, l3_r, agg_r,
     out_h,
-    load_v, stiff_v, inv_v, out_v, in_sem, out_sem,
+    load_v, stiff_v, inv_v, in_sem,
     es, er, es_sem, er_sem,
     ps, pr, ps_sem, pr_sem, pbig, pbigb, pplain,
     ns, nr, ns_sem, nr_sem,
@@ -85,13 +85,15 @@
         jnp.where(lane < width, ew[0], ew[1]),
         jnp.where(lane < 3 * width, ew[2], ew[3]),
     )
-    bases = (0, 128, 384, 512)
+    hw = total // 2
+    bases = (0, 128, hw, hw + 128)
+    wx, wy = wrow[:, :hw], wrow[:, hw:]
     lane128 = lax.broadcasted_iota(jnp.int32, (1, 128), 1)
     low = lane128 < 64
     low192 = lax.broadcasted_iota(jnp.int32, (1, 256), 1) < 192
 
     def aligned(x, e):
-        part = x[:, bases[e]:bases[e] + 256]
+        part = x[:, 128 * (e % 2):128 * (e % 2) + 256]
         return pltpu.roll(part, 192, 1) if e % 2 else part
 
     def put_back(part, e):
@@ -117,9 +119,9 @@
             device_id=near(e), device_id_type=MESH,
         )
 
-    def send_edges(x, k, value):
-        for e in (2, 3, 0, 1):
-            a, b = pack(value, e)
+    def send_edges(x, k, part, s):
+        for e in (2 * s, 2 * s + 1):
+            a, b = pack(part, e)
             es[x, k, e, :R] = a.astype(BF16)
             es[x, k, e, R:] = b.astype(BF16)
 
@@ -127,24 +129,19 @@
             def _():
                 edge_copy(x, k, e).start()
 
-    def wait_edges(x, k):
-        for e in (0, 1, 2, 3):
+    def with_edges(x, k, part, s):
+        added = []
+        for e in (2 * s, 2 * s + 1):
             @pl.when(exists[e])
             def _():
                 edge_wait(x, k, e).wait_recv()
-
-    def with_edges(x, k, value):
-        added = []
-        for e in range(4):
+        for e in (2 * s, 2 * s + 1):
             a = er[x, k, e, :R].astype(F32)
             b = er[x, k, e, R:].astype(F32)
             b = jnp.concatenate([b, pltpu.roll(b, 64, 1)], axis=0)
             added.append(put_back(jnp.concatenate([a, b], axis=1), e))
-        parts = []
-        for s in range(2):
-            first, second = added[2 * s], added[2 * s + 1]
-            parts += [first[:, :128], first[:, 128:] + second[:, :128], second[:, 128:]]
-        return value + jnp.concatenate(parts, axis=1)
+        first, second = added
+        return part + jnp.concatenate([first[:, :128], first[:, 128:] + second[:, :128], second[:, 128:]], axis=1)
 
     phi = phi_r[0, 0]
     phi_hi = phi.astype(BF16)
@@ -156,7 +153,7 @@
     pbig[...] = jnp.zeros_like(pbig)
     pbig[0:prow, :] = pown
     for e in range(4):
-        ps[e] = aligned(pown, e)
+        ps[e] = aligned(pown[:, hw * (e // 2):hw * (e // 2) + hw], e)
 
     def base_copy(e, there):
         return pltpu.make_async_remote_copy(
@@ -207,7 +204,7 @@
 
     def fold(v):
         acc = v[:, :128]
-        for i in range(128, total, 128):
+        for i in range(128, v.shape[1], 128):
             acc = acc + v[:, i:i + 128]
         return acc
 
@@ -251,33 +248,43 @@
         return [c[:, 128 * q:128 * q + 128] for q in range(n)]
 
     def wide(c):
-        return jnp.concatenate([c] * (total // 128), axis=1)
+        return jnp.concatenate([c] * (hw // 128), axis=1)
 
     def start(k):
         load_copy(k).wait()
-        send_edges(0, k, load_v[pl.ds(k * R, R), :])
+        v = load_v[pl.ds(k * R, R), :]
+        send_edges(0, k, v[:, hw:], 1)
+        send_edges(0, k, v[:, :hw], 0)
 
     def solve_coarse(t, k, c):
         cown[t, k] = c
         cg[t, k, row] = jnp.concatenate([c * m for m in masks], axis=0)
         spread(cg, cg_ss, cg_rs, t, k, "gy")
 
-    def local_part(t, k, r, rsb):
-        u = wrow * dot(rsb, inv_v[...], NN)
-        send_edges(1 + 2 * t, k, u)
-        ur[t, k] = u
-        gp[t, k] = fold(r * u)
+    def local_rest(t, k, rx, ry, sy, acc):
+        uy = wy * (acc[:, hw:] + dot(sy, inv_v[hw:, hw:], NN))
+        send_edges(1 + 2 * t, k, uy, 1)
+        ux = wx * (acc[:, :hw] + dot(sy, inv_v[hw:, :hw], NN))
+        send_edges(1 + 2 * t, k, ux, 0)
+        ur[t, k, :, hw:] = uy
+        ur[t, k, :, :hw] = ux
+        gp[t, k] = fold(rx * ux) + fold(ry * uy)
 
     def first_local(k):
-        wait_edges(0, k)
-        r = with_edges(0, k, load_v[pl.ds(k * R, R), :])
-        rsb = (wrow * r).astype(BF16)
-        c = dot(phi2, rsb, NT)
-        solve_coarse(0, k, c[:prim] + c[prim:])
-        rr[k] = r
+        v = load_v[pl.ds(k * R, R), :]
+        rx = with_edges(0, k, v[:, :hw], 0)
+        sx = (wx * rx).astype(BF16)
+        rr[k, :, :hw] = rx
         if k == 0:
             inv_copy.wait()
-        local_part(0, k, r, rsb)
+        c = dot(phi2[:, :hw], sx, NT)
+        acc = dot(sx, inv_v[:hw, :], NN)
+        ry = with_edges(0, k, v[:, hw:], 1)
+        sy = (wy * ry).astype(BF16)
+        rr[k, :, hw:] = ry
+        c = c + dot(phi2[:, hw:], sy, NT)
+        solve_coarse(0, k, c[:prim] + c[prim:])
+        local_rest(0, k, rx, ry, sy, acc)
 
     def middle(t, k):
         gathered(cg, cg_ss, cg_rs, t, k, "gy")
@@ -344,9 +351,10 @@
             c = cown[0, k] - alpha * c
         coarse = dot(x.astype(BF16), pbigb[...], TN)
         extra = jnp.sum(c * full, axis=0, keepdims=True)
-        wait_edges(1 + 2 * t, k)
-        z = with_edges(1 + 2 * t, k, ur[t, k] + coarse)
-        return z, extra
+        z = [
+            with_edges(1 + 2 * t, k, ur[t, k, :, s * hw:s * hw + hw] + coarse[:, s * hw:s * hw + hw], s) for s in range(2)
+        ]
+        return jnp.concatenate(z, axis=1), extra
 
     def message(t, k, parts, extra):
         sa[t, k, row] = tile_of(parts, extra)
@@ -376,7 +384,8 @@
             @pl.when(exists[e])
             def _():
                 coarse_copy(k, e, e ^ 1).start()
-        send_edges(2, k, y)
+        send_edges(2, k, y[:, hw:], 1)
+        send_edges(2, k, y[:, :hw], 0)
 
     def coarse_start(k):
         c = cown[1, k]
@@ -415,12 +424,10 @@
         tot[k, 1:2] = delta
         tot[k, 2:3] = rate
         alpha, = columns_of([rate])
-        wait_edges(2, k)
-        r = rr[k] - wide(alpha) * with_edges(2, k, y0r[k])
-        local_part(1, k, r, (wrow * r).astype(BF16))
-
-    def out_copy(k):
-        return pltpu.make_async_copy(out_v.at[pl.ds(k * R, R)], out_h.at[0, 0, pl.ds(k * R, R)], out_sem.at[k])
+        rx = rr[k, :, :hw] - wide(alpha) * with_edges(2, k, y0r[k, :, :hw], 0)
+        acc = dot((wx * rx).astype(BF16), inv_v[:hw, :], NN)
+        ry = rr[k, :, hw:] - wide(alpha) * with_edges(2, k, y0r[k, :, hw:], 1)
+        local_rest(1, k, rx, ry, (wy * ry).astype(BF16), acc)
 
     def finish(k):
         gamma, delta, rate = tot[k, 0:1], tot[k, 1:2], tot[k, 2:3]
@@ -428,8 +435,9 @@
         beta = new / gamma
         alpha1 = new / (along + beta * across + beta * beta * delta)
         first, second = columns_of([rate + alpha1 * beta, alpha1])
-        out_v[pl.ds(k * R, R), :] = wide(first) * z0r[k] + wide(second) * z1r[k]
-        out_copy(k).start()
+        for s in range(2):
+            here = slice(s * hw, s * hw + hw)
+            out_h[0, 0, pl.ds(k * R, R), here] = wide(first) * z0r[k, :, here] + wide(second) * z1r[k, :, here]
 
     steps = [
         start, first_local, functools.partial(middle, 0), first_apply, functools.partial(relay, 0), coarse_start,
@@ -440,7 +448,6 @@
             step(k)
 
     for k in range(CHUNKS):
-        out_copy(k).wait()
         for e in range(4):
             @pl.when(exists[e])
             def _():
@@ -470,8 +477,8 @@
     anyw = pl.BlockSpec(memory_space=pl.ANY)
     here = pl.BlockSpec(memory_space=pltpu.VMEM)
     scratch = [
-        vmem((rows, total), F32), vmem((total, total), BF16), vmem((total, total), BF16), vmem((rows, total), F32),
-        dma((2 + C,)), dma((C,)),
+        vmem((rows, total), F32), vmem((total, total), BF16), vmem((total, total), BF16),
+        dma((2 + C,)),
         vmem((4, C, 4, R + R // 2, 128), BF16), vmem((4, C, 4, R + R // 2, 128), BF16), dma((4, C, 4)), dma((4, C, 4)),
         vmem((4, prow, 256), F32), vmem((4, prow, 256), F32), dma((4,)), dma((4,)), vmem((5 * prow, total), F32),
         vmem((5 * prow, total), BF16), vmem((5 * prim, total), BF16),
@@ -488,9 +495,9 @@
     ]
     return pl.pallas_call(
         functools.partial(kernel, ngx, ngy, rows, total, prim),
-        out_shape=jax.ShapeDtypeStruct((1, 1, rows, total), F32),
+        out_shape=pltpu.VMEM((1, 1, rows, total), F32),
         in_specs=[anyw, anyw, anyw, here, here, here, pl.BlockSpec(memory_space=pltpu.SMEM)],
-        out_specs=anyw,
+        out_specs=here,
         scratch_shapes=scratch,
         compiler_params=pltpu.CompilerParams(
             collective_id=0, has_side_effects=True, vmem_limit_bytes=60 * 1024 * 1024

time: 55.5 us -> 52.1 us (0.939)
  Pallas kernels: 52.4 us -> 50.3 us
  local copies, waits for them, and re-layouts: 2.21 us -> 0.95 us
    pallas_call x1, Pallas kernels: 52.4 us -> 50.3 us  [body(): pl.pallas_call(functools.partial(kernel, ngx, ngy, rows, total, prim), ou...]
    unnamed x1, local copies, waits for them, and re-layouts: 2.21 us -> 0.95 us
where the time goes in v3:
time: 52.1 us; the launch traced here: 51.9 us
  Pallas kernels  50.3 us (97%)
  local copies, waits for them, and re-layouts  0.95 us (2%)
  between operations  0.66 us (1%)
    pallas_call x1, Pallas kernels, body(): pl.pallas_call(functools.partial(kernel, ngx, ngy, rows, total, prim), ou...  50.3 us

profile of v3, /device:TPU:0, one launch (start us, length us, event | category | flops | bytes accessed | tf_op | source)
XLA Modules:
  0.0 51.9 jit_solution(13898530347731776241)
XLA Ops:
  0.7 50.3 %shard_map.73 = f32[1,1,320,768]{3,2,1,0:T(8,128)S(1)} custom-call(f32[1,1,320,768]{3,2,1,0:T(8,128)} %load_h.1, bf16[1,1,768,768]{3,2,1,0:T(8,128)(2,1)} %stiff_h.1, bf16[1,1,768,768]{3,2,1,0:T(8,128)(2,1)} %inv_h.1, f32[1,1,8,768]{3,2,1,0:T(8,128)} %phi_r.1, f32[1,32,32]{2,1,0:T(8,128)} %l2_r.1, bf16[128,128]{1,0:T(8,128)(2,1)} %l3_r.1, s32[1,1]{1,0:T(1,128)S(6)} %copy.10.agg_r), custom_call_target="tpu_custom_call" | custom-call | tf_op jit(solution)/shard_map/pallas_call | solution.py:496
  51.0 0.9 %copy.9 = f32[1,1,320,768]{3,2,1,0:T(8,128)} copy(f32[1,1,320,768]{3,2,1,0:T(8,128)S(1)} %shard_map.73) | data formatting | bytes 1966080

commit v4 on v3

--- a/solution.py
+++ b/solution.py
@@ -38,7 +38,7 @@
     cg, cg_ss, cg_rs, eg, eg_ss, eg_rs, xs, xr, xs_sem, xr_sem,
     x2s, t3s,
     sa, sa_ss, sa_rs, sb, sb_ss, sb_rs,
-    rr, ur, z0r, z1r, y0r, gp, cown, xown, xall, xfull, tot,
+    rr, ur, z0r, z1r, y0r, gp, cown, xown, acol, xfull, tot,
 ):
     width = total // 4
     R = rows // CHUNKS
@@ -268,7 +268,8 @@
         send_edges(1 + 2 * t, k, ux, 0)
         ur[t, k, :, hw:] = uy
         ur[t, k, :, :hw] = ux
-        gp[t, k] = fold(rx * ux) + fold(ry * uy)
+        if t == 0:
+            gp[t, k] = fold(rx * ux) + fold(ry * uy)
 
     def first_local(k):
         v = load_v[pl.ds(k * R, R), :]
@@ -342,11 +343,9 @@
             full = full + m * here[q * prim:(q + 1) * prim]
         c = cown[t, k]
         if t == 0:
-            xall[k] = x
             xfull[k] = full
         else:
             alpha = tot[k, 2:3]
-            x = xall[k] - alpha * x
             full = xfull[k] - alpha * full
             c = cown[0, k] - alpha * c
         coarse = dot(x.astype(BF16), pbigb[...], TN)
@@ -398,6 +397,8 @@
 
     def second_apply(k):
         z, extra = direction(1, k)
+        a = wide(acol[k])
+        z = z0r[k] - jnp.concatenate([a, a], axis=1) * z
         y = dot(z.astype(BF16), stiff_v[...], NN)
         message(1, k, [gp[1, k], fold(z * y), fold(z * y0r[k] + z0r[k] * y)], extra)
         z1r[k] = z
@@ -418,16 +419,28 @@
         return rows_from(s, 2 + t)
 
     def second_local(k):
+        rows_k = pl.ds(k * R, R)
+        sx = with_edges(2, k, y0r[k, :, :hw], 0)
+        load_v[rows_k, :hw] = sx
+        acc = dot((wx * sx).astype(BF16), inv_v[:hw, :], NN)
+        sy = with_edges(2, k, y0r[k, :, hw:], 1)
+        load_v[rows_k, hw:] = sy
+        local_rest(1, k, sx, sy, (wy * sy).astype(BF16), acc)
+
+    def first_rate(k):
         gamma, delta = summed(0, k)
         rate = gamma / delta
         tot[k, 0:1] = gamma
         tot[k, 1:2] = delta
         tot[k, 2:3] = rate
         alpha, = columns_of([rate])
-        rx = rr[k, :, :hw] - wide(alpha) * with_edges(2, k, y0r[k, :, :hw], 0)
-        acc = dot((wx * rx).astype(BF16), inv_v[:hw, :], NN)
-        ry = rr[k, :, hw:] - wide(alpha) * with_edges(2, k, y0r[k, :, hw:], 1)
-        local_rest(1, k, rx, ry, (wy * ry).astype(BF16), acc)
+        acol[k] = alpha
+        part = jnp.zeros((R, 128), F32)
+        for s in range(2):
+            at = slice(s * hw, s * hw + hw)
+            a = wide(alpha)
+            part = part + fold((rr[k, :, at] - a * load_v[pl.ds(k * R, R), at]) * (ur[0, k, :, at] - a * ur[1, k, :, at]))
+        gp[1, k] = part
 
     def finish(k):
         gamma, delta, rate = tot[k, 0:1], tot[k, 1:2], tot[k, 2:3]
@@ -441,7 +454,7 @@
 
     steps = [
         start, first_local, functools.partial(middle, 0), first_apply, functools.partial(relay, 0), coarse_start,
-        second_local, functools.partial(middle, 1), second_apply, functools.partial(relay, 1), finish,
+        second_local, functools.partial(middle, 1), first_rate, second_apply, functools.partial(relay, 1), finish,
     ]
     for index, step in enumerate(steps):
         for k in range(CHUNKS):
@@ -491,7 +504,7 @@
         vmem((2, C, ngx, 8, 128), F32), dma((2, C, ngx)), dma((2, C, ngx)),
         vmem((C, R, total), F32), vmem((2, C, R, total), F32), vmem((C, R, total), F32), vmem((C, R, total), F32),
         vmem((C, R, total), F32), vmem((2, C, R, 128), F32), vmem((2, C, prim, R), F32), vmem((2, C, 3, prim, R), F32),
-        vmem((C, 5 * prow, R), F32), vmem((C, prim, R), F32), vmem((C, 8, R), F32),
+        vmem((C, R, 128), F32), vmem((C, prim, R), F32), vmem((C, 8, R), F32),
     ]
     return pl.pallas_call(
         functools.partial(kernel, ngx, ngy, rows, total, prim),

time: 52.1 us -> 50.4 us (0.967)
  Pallas kernels: 50.3 us -> 48.6 us
    pallas_call x1, Pallas kernels: 50.3 us -> 48.6 us  [body(): pl.pallas_call(functools.partial(kernel, ngx, ngy, rows, total, prim), ou...]
where the time goes in v4:
time: 50.4 us; the launch traced here: 50.2 us
  Pallas kernels  48.6 us (96%)
  local copies, waits for them, and re-layouts  0.95 us (2%)
  between operations  0.66 us (1%)
    pallas_call x1, Pallas kernels, body(): pl.pallas_call(functools.partial(kernel, ngx, ngy, rows, total, prim), ou...  48.6 us

profile of v4, /device:TPU:0, one launch (start us, length us, event | category | flops | bytes accessed | tf_op | source)
XLA Modules:
  0.0 50.2 jit_solution(11968175384973745121)
XLA Ops:
  0.7 48.6 %shard_map.73 = f32[1,1,320,768]{3,2,1,0:T(8,128)S(1)} custom-call(f32[1,1,320,768]{3,2,1,0:T(8,128)} %load_h.1, bf16[1,1,768,768]{3,2,1,0:T(8,128)(2,1)} %stiff_h.1, bf16[1,1,768,768]{3,2,1,0:T(8,128)(2,1)} %inv_h.1, f32[1,1,8,768]{3,2,1,0:T(8,128)} %phi_r.1, f32[1,32,32]{2,1,0:T(8,128)} %l2_r.1, bf16[128,128]{1,0:T(8,128)(2,1)} %l3_r.1, s32[1,1]{1,0:T(1,128)S(6)} %copy.10.agg_r), custom_call_target="tpu_custom_call" | custom-call | tf_op jit(solution)/shard_map/pallas_call | solution.py:509
  49.2 0.9 %copy.9 = f32[1,1,320,768]{3,2,1,0:T(8,128)} copy(f32[1,1,320,768]{3,2,1,0:T(8,128)S(1)} %shard_map.73) | data formatting | bytes 1966080
